TPU v7x, 32 devices: a whole 2x2x4 slice. The times are simulated.
32 devices in a mesh: section: 2 (over x), seq: 16 (over z, y, core).
Axes of the slice: x: 2, y: 2, z: 4, core: 2. Of those that a mesh axis runs over, the one named last changes fastest.
Arguments:
- prev_out: bfloat16 [2, 2048, 1792], P('section', 'seq'), may hold values from -6 to 6
- prev_grad: bfloat16 [2, 2048, 1792], P('section', 'seq'), may hold values from -6 to 6
- saved_in: bfloat16 [2, 2048, 1792], P('section', 'seq'), may hold values from -6 to 6
- seq_mix: bfloat16 [2, 128, 128], P('section'), may hold values from -0.5 to 0.5
- coeffs: float32 [2, 4, 4, 1792], P('section'), may hold values from -1 to 1
- mixer: bfloat16 [2, 1792, 448], P('section'), may hold values from -0.25 to 0.25
Outputs:
- out_fwd: bfloat16 [2, 2048, 1792], P('section', 'seq')
- out_dh: bfloat16 [2, 2048, 1792], P('section', 'seq')
- grad_w: float32 [2, 1792, 448], P('section', 'seq')
- grad_b: float32 [2, 128, 128], P('section')
All inputs are finite; a program needn't handle non-finite values.
Results may differ from a plain program's by a relative error of at most 0.01.
Values may be sent and summed in bfloat16 or wider, within the bound.
No kernel may reach another device: no remote copies, remote signals or barrier semaphores. Data moves between devices by JAX's collectives and lax.ppermute only.
A program may use at most 64 MiB of HBM per device.

v0:
```python
import jax
import jax.numpy as jnp
from jax import lax
from jax.sharding import PartitionSpec as P


def swapped(block, axis, stride):
    count = lax.axis_size(axis)
    route = []
    for low in range(count):
        high = low | 1 << stride
        if high != low and high < count:
            route += [(low, high), (high, low)]
    return lax.ppermute(block, axis, route)


def from_behind(block, axis, distance):
    devices = range(lax.axis_size(axis))
    route = [((i - distance) % len(devices), i) for i in devices]
    return lax.ppermute(block, axis, route)


def mix_forward(state, factors):
    position = lax.axis_index("seq")
    number = lax.axis_size("seq").bit_length() - 1
    for bit_level in range(number):
        partner = swapped(state, "seq", bit_level)
        upper_side = jnp.bitwise_and(jnp.right_shift(position, bit_level), 1) == 1
        own_vals = state.astype(jnp.float32)
        partner_vals = partner.astype(jnp.float32)
        as_lower = factors[bit_level, 0] * own_vals + factors[bit_level, 1] * partner_vals
        as_upper = factors[bit_level, 2] * partner_vals + factors[bit_level, 3] * own_vals
        state = jnp.where(upper_side, as_upper, as_lower).astype(jnp.bfloat16)
    return state


def mix_adjoint(state, factors):
    position = lax.axis_index("seq")
    number = lax.axis_size("seq").bit_length() - 1
    for bit_level in reversed(range(number)):
        partner = swapped(state, "seq", bit_level)
        upper_side = jnp.bitwise_and(jnp.right_shift(position, bit_level), 1) == 1
        own_vals = state.astype(jnp.float32)
        partner_vals = partner.astype(jnp.float32)
        as_lower = factors[bit_level, 0] * own_vals + factors[bit_level, 2] * partner_vals
        as_upper = factors[bit_level, 1] * partner_vals + factors[bit_level, 3] * own_vals
        state = jnp.where(upper_side, as_upper, as_lower).astype(jnp.bfloat16)
    return state


def block_apply(rows, blocks):
    block_len = blocks.shape[0]
    shaped = rows.reshape(-1, block_len, rows.shape[1])
    mixed = jnp.einsum("ij,bjd->bid", blocks, shaped, preferred_element_type=jnp.float32)
    return mixed.reshape(rows.shape).astype(jnp.bfloat16)


def layer_forward(rows, blocks, factors, weights):
    width = rows.shape[1]
    block_width = weights.shape[1]
    nblocks = width // block_width
    blocked = block_apply(rows, blocks)
    state = mix_forward(blocked, factors)
    act = (rows.astype(jnp.float32) + state.astype(jnp.float32)).astype(jnp.bfloat16)
    act3 = act.reshape(-1, nblocks, block_width)
    weight3 = weights.reshape(nblocks, block_width, block_width)
    pre = jnp.einsum("tbi,bio->tbo", act3, weight3, preferred_element_type=jnp.float32)
    return (act3, pre)


def on_device(prev_out, prev_grad, saved_in, seq_mix, coeffs, mixer):
    incoming = from_behind(prev_out, "section", 1)[0]
    upstream = from_behind(prev_grad, "section", -1)[0]
    blocks = seq_mix[0]
    factors = coeffs[0]
    weights = mixer[0]
    rows_dev, width = incoming.shape
    block_width = weights.shape[1]
    nblocks = width // block_width
    block_len = blocks.shape[0]
    act3, pre = layer_forward(incoming, blocks, factors, weights)
    result = (
        (act3.astype(jnp.float32) + jax.nn.silu(pre)).reshape(rows_dev, width).astype(jnp.bfloat16)
    )
    stored = saved_in[0]
    act_two, pre_two = layer_forward(stored, blocks, factors, weights)
    sigma = jax.nn.sigmoid(pre_two)
    gz = (
        upstream.astype(jnp.float32).reshape(-1, nblocks, block_width)
        * (sigma * (1.0 + pre_two * (1.0 - sigma)))
    ).astype(jnp.bfloat16)
    weight3 = weights.reshape(nblocks, block_width, block_width)
    back = jnp.einsum("tbo,bio->tbi", gz, weight3, preferred_element_type=jnp.float32)
    d_act = (upstream.astype(jnp.float32) + back.reshape(rows_dev, width)).astype(jnp.bfloat16)
    weight_term = jnp.einsum(
        "tbi,tbo->bio", act_two, gz, preferred_element_type=jnp.float32
    ).reshape(width, block_width)
    grad_weight = lax.psum_scatter(weight_term, "seq", scatter_dimension=0, tiled=True)
    dblocked = mix_adjoint(d_act, factors)
    dblk = dblocked.reshape(-1, block_len, width)
    stored_blk = stored.reshape(-1, block_len, width)
    block_term = jnp.einsum("bid,bjd->ij", dblk, stored_blk, preferred_element_type=jnp.float32)
    grad_block = lax.psum(block_term, "seq")
    through = jnp.einsum("ij,bid->bjd", blocks, dblk, preferred_element_type=jnp.float32).reshape(
        rows_dev, width
    )
    in_grad = (d_act.astype(jnp.float32) + through).astype(jnp.bfloat16)
    return (result[None], in_grad[None], grad_weight[None], grad_block[None])


def solution(mesh):
    placed = (
        P("section", "seq", None),
        P("section", "seq", None),
        P("section", "seq", None),
        P("section", None, None),
        P("section", None, None, None),
        P("section", None, None),
    )
    return jax.shard_map(
        on_device,
        mesh=mesh,
        in_specs=placed,
        out_specs=(
            P("section", "seq", None),
            P("section", "seq", None),
            P("section", "seq", None),
            P("section", None, None),
        ),
        check_vma=False,
    )
```

profile of v0, /device:TPU:0, one launch (start us, length us, event | category | flops | bytes accessed | tf_op | source)
XLA Modules:
  0.0 301.7 jit_solution(15228928650524788524)
XLA Ops:
  7.2 0.7 copy-done
  7.9 1.3 fusion.1
  9.8 1.3 slice_reduce_fusion.15
  11.2 1.3 fusion.20
  12.6 3.0 collective-permute-start.7
  15.5 10.8 %collective-permute-done.7 = bf16[128,1792]{0,1:T(8,128)(2,1)S(1)} collective-permute-done((bf16[128,1792]{0,1:T(8,128)(2,1)S(1)}, bf16[128,1792]{0,1:T(8,128)(2,1)S(1)}, u32[]{:S(2)}, u32[]{:S(2)}) %collective-permute-start.7) | collective-permute-done | bytes 458784 | tf_op jit(solution)/shard_map/ppermute | solution.py:14
  26.4 1.3 fusion.24
  27.7 1.9 collective-permute-start.8
  29.6 10.3 %collective-permute-done.8 = bf16[128,1792]{0,1:T(8,128)(2,1)S(1)} collective-permute-done((bf16[128,1792]{0,1:T(8,128)(2,1)S(1)}, bf16[128,1792]{0,1:T(8,128)(2,1)S(1)}, u32[]{:S(2)}, u32[]{:S(2)}) %collective-permute-start.8) | collective-permute-done | bytes 458784 | tf_op jit(solution)/shard_map/ppermute | solution.py:14
  39.8 1.3 fusion.28
  41.2 2.6 collective-permute-start.9
  43.7 1.0 copy.12
  44.7 1.5 collective-permute-start.5
  46.2 1.0 copy.13
  47.2 2.8 copy.18
  50.0 13.3 %collective-permute-done.9 = bf16[128,1792]{0,1:T(8,128)(2,1)} collective-permute-done((bf16[128,1792]{0,1:T(8,128)(2,1)S(1)}, bf16[128,1792]{0,1:T(8,128)(2,1)}, u32[]{:S(2)}, u32[]{:S(2)}) %collective-permute-start.9) | collective-permute-done | bytes 458784 | tf_op jit(solution)/shard_map/ppermute | solution.py:14
  63.2 3.0 add_convert_fusion.1
  66.2 0.8 convolution_bitcast_fusion.1
  67.1 0.7 fusion.59
  68.0 0.9 copy-done.4
  69.1 22.5 %collective-permute-done.10 = bf16[128,1792]{0,1:T(8,128)(2,1)S(1)} collective-permute-done((bf16[128,1792]{0,1:T(8,128)(2,1)S(1)}, bf16[128,1792]{0,1:T(8,128)(2,1)S(1)}, u32[]{:S(2)}, u32[]{:S(2)}) %collective-permute-start.10) | collective-permute-done | bytes 458784 | tf_op jit(solution)/shard_map/ppermute | solution.py:14
  91.6 2.2 fusion.36
  93.8 2.0 copy.10
  95.8 0.6 collective-permute-start
  96.4 9.0 %collective-permute-done.11 = bf16[128,1792]{0,1:T(8,128)(2,1)} collective-permute-done((bf16[128,1792]{0,1:T(8,128)(2,1)}, bf16[128,1792]{0,1:T(8,128)(2,1)}, u32[]{:S(2)}, u32[]{:S(2)}) %collective-permute-start.11) | collective-permute-done | bytes 458784 | tf_op jit(solution)/shard_map/ppermute | solution.py:14
  105.5 2.9 fusion.40
  108.8 10.0 %collective-permute-done.12 = bf16[128,1792]{0,1:T(8,128)(2,1)S(1)} collective-permute-done((bf16[128,1792]{0,1:T(8,128)(2,1)S(1)}, bf16[128,1792]{0,1:T(8,128)(2,1)S(1)}, u32[]{:S(2)}, u32[]{:S(2)}) %collective-permute-start.12) | collective-permute-done | bytes 458784 | tf_op jit(solution)/shard_map/ppermute | solution.py:14
  118.8 1.3 fusion.44
  120.3 1.8 collective-permute-done.13
  122.0 2.2 fusion.48
  124.3 0.8 copy-done.2
  125.0 1.0 convolution_bitcast_fusion.3
  126.3 3.7 %fusion.58 = f32[4,448,448]{2,1,0:T(8,128)} fusion(bf16[128,4,448]{0,2,1:T(8,128)(2,1)S(1)} %bitcast.83, f32[128,4,448]{0,2,1:T(8,128)} %copy-done.6, bf16[128,4,448]{0,2,1:T(8,128)(2,1)S(1)} %bitcast.81), kind=kOutput, calls=%fused_computation.135 | convolution fusion | flops 207814656 | bytes 5046272 | tf_op jit(solution)/shard_map/tbi,tbo->bio/dot_general | solution.py:95
  130.0 1.0 copy-done.9
  131.3 12.5 %collective-permute-done.2 = bf16[128,1792]{0,1:T(8,128)(2,1)S(1)} collective-permute-done((bf16[128,1792]{0,1:T(8,128)(2,1)S(1)}, bf16[128,1792]{0,1:T(8,128)(2,1)S(1)}, u32[]{:S(2)}, u32[]{:S(2)}) %collective-permute-start.2) | collective-permute-done | bytes 458784 | tf_op jit(solution)/shard_map/ppermute | solution.py:14
  143.7 1.3 fusion.8
  145.1 0.6 collective-permute-start.3
  146.0 11.1 %collective-permute-done.3 = bf16[128,1792]{0,1:T(8,128)(2,1)S(1)} collective-permute-done((bf16[128,1792]{0,1:T(8,128)(2,1)S(1)}, bf16[128,1792]{0,1:T(8,128)(2,1)S(1)}, u32[]{:S(2)}, u32[]{:S(2)}) %collective-permute-start.3) | collective-permute-done | bytes 458784 | tf_op jit(solution)/shard_map/ppermute | solution.py:14
  157.1 2.2 fusion.12
  159.3 2.6 collective-permute-start.4
  162.1 1.0 copy.17
  163.1 18.6 %collective-permute-done.4 = bf16[128,1792]{0,1:T(8,128)(2,1)} collective-permute-done((bf16[128,1792]{0,1:T(8,128)(2,1)}, bf16[128,1792]{0,1:T(8,128)(2,1)}, u32[]{:S(2)}, u32[]{:S(2)}) %collective-permute-start.4) | collective-permute-done | bytes 458784 | tf_op jit(solution)/shard_map/ppermute | solution.py:14
  181.7 2.9 add_convert_fusion.3
  184.5 0.9 add_convert_fusion.2
  185.4 1.0 copy.16
  186.4 31.9 %all-reduce.2.cloned.1.call-done = f32[1,128,128]{2,1,0:T(8,128)} async-done(((f32[1,128,128]{2,1,0:T(8,128)}), f32[1,128,128]{2,1,0:T(8,128)}) %all-reduce.2.cloned.1.call-update) | async-done | bytes 65552 | tf_op jit(solution)/shard_map/psum | solution.py:103
  218.3 75.1 %reduce-scatter.2.cloned.1.call-done = f32[112,448]{1,0:T(8,128)} async-done(((f32[1792,448]{1,0:T(8,128)}), f32[112,448]{1,0:T(8,128)}) %reduce-scatter.2.cloned.1.call-update) | async-done | bytes 200720 | tf_op jit(solution)/shard_map/reduce_scatter | solution.py:98
  293.4 1.5 copy.20
  (39 shorter events, 2.5 us)
Async XLA Ops:
  7.2 0.8 copy-start
  7.2 211.1 %all-reduce.2.cloned.1.call-start = ((), (), s32[]{:S(2)}) async-start(), calls=%async_computation.2 | async-start | bytes 131072 | tf_op jit(solution)/shard_map/psum | solution.py:103
  9.3 2.0 collective-permute-start.6
  11.2 32.5 %copy-start.11 = (bf16[1,128,1792]{2,1,0:T(8,128)(2,1)S(1)}, bf16[1,128,1792]{2,1,0:T(8,128)(2,1)}, u32[]{:S(2)}) copy-start(bf16[1,128,1792]{2,1,0:T(8,128)(2,1)} %param.7) | copy-start | bytes 1376260
  12.6 13.8 %collective-permute-start.7 = (bf16[128,1792]{0,1:T(8,128)(2,1)S(1)}, bf16[128,1792]{0,1:T(8,128)(2,1)S(1)}, u32[]{:S(2)}, u32[]{:S(2)}) collective-permute-start(bf16[128,1792]{0,1:T(8,128)(2,1)S(1)} %fusion.20), channel_id=1, source_target_pairs={{0,2},{2,0},{1,3},{3,1},{4,6},{6,4},{5,7},{7,5},{8,10},{10,8},{9,1... | collective-permute-start | bytes 1376264 | tf_op jit(solution)/shard_map/ppermute | solution.py:14
  26.3 19.9 %copy-start.1 = (bf16[1,128,1792]{2,1,0:T(8,128)(2,1)S(1)}, bf16[1,128,1792]{2,1,0:T(8,128)(2,1)}, u32[]{:S(2)}) copy-start(bf16[1,128,1792]{2,1,0:T(8,128)(2,1)} %param.8) | copy-start | bytes 1376260
  27.7 12.1 %collective-permute-start.8 = (bf16[128,1792]{0,1:T(8,128)(2,1)S(1)}, bf16[128,1792]{0,1:T(8,128)(2,1)S(1)}, u32[]{:S(2)}, u32[]{:S(2)}) collective-permute-start(bf16[128,1792]{0,1:T(8,128)(2,1)S(1)} %fusion.24), channel_id=1, source_target_pairs={{0,4},{4,0},{1,5},{5,1},{2,6},{6,2},{3,7},{7,3},{8,12},{12,8},{9,1... | collective-permute-start | bytes 1376264 | tf_op jit(solution)/shard_map/ppermute | solution.py:14
  41.2 8.8 %copy-start.10 = (bf16[128,1792]{0,1:T(8,128)(2,1)}, bf16[128,1792]{0,1:T(8,128)(2,1)S(1)}, u32[]{:S(2)}) copy-start(bf16[128,1792]{0,1:T(8,128)(2,1)S(1)} %fusion.28) | copy-start | bytes 1376260
  41.2 22.1 %collective-permute-start.9 = (bf16[128,1792]{0,1:T(8,128)(2,1)S(1)}, bf16[128,1792]{0,1:T(8,128)(2,1)}, u32[]{:S(2)}, u32[]{:S(2)}) collective-permute-start(bf16[128,1792]{0,1:T(8,128)(2,1)S(1)} %fusion.28), channel_id=1, source_target_pairs={{0,8},{8,0},{1,9},{9,1},{2,10},{10,2},{3,11},{11,3},{4,12},{12,4},... | collective-permute-start | bytes 1376264 | tf_op jit(solution)/shard_map/ppermute | solution.py:14
  44.7 22.4 %collective-permute-start.5 = (bf16[1,128,1792]{1,2,0:T(8,128)(2,1)}, bf16[1,128,1792]{1,2,0:T(8,128)(2,1)S(1)}, u32[]{:S(2)}, u32[]{:S(2)}) collective-permute-start(bf16[1,128,1792]{1,2,0:T(8,128)(2,1)} %copy.12), channel_id=1, source_target_pairs={{16,0},{0,16},{17,1},{1,17},{18,2},{2,18},{19,3},{3,19},{20,4},{4,... | collective-permute-start | bytes 1376264 | tf_op jit(solution)/shard_map/ppermute | solution.py:20
  67.1 0.9 copy-start.6
  68.0 0.9 copy-start.4
  69.0 22.6 %collective-permute-start.10 = (bf16[128,1792]{0,1:T(8,128)(2,1)S(1)}, bf16[128,1792]{0,1:T(8,128)(2,1)S(1)}, u32[]{:S(2)}, u32[]{:S(2)}) collective-permute-start(bf16[128,1792]{0,1:T(8,128)(2,1)S(1)} %fusion.50), channel_id=1, source_target_pairs={{0,8},{8,0},{1,9},{9,1},{2,10},{10,2},{3,11},{11,3},{4,12},{12,4},... | collective-permute-start | bytes 1376264 | tf_op jit(solution)/shard_map/ppermute | solution.py:14
  93.8 11.6 %collective-permute-start.11 = (bf16[128,1792]{0,1:T(8,128)(2,1)}, bf16[128,1792]{0,1:T(8,128)(2,1)}, u32[]{:S(2)}, u32[]{:S(2)}) collective-permute-start(bf16[128,1792]{0,1:T(8,128)(2,1)} %fusion.36), channel_id=1, source_target_pairs={{0,4},{4,0},{1,5},{5,1},{2,6},{6,2},{3,7},{7,3},{8,12},{12,8},{9,1... | collective-permute-start | bytes 1376264 | tf_op jit(solution)/shard_map/ppermute | solution.py:14
  95.8 12.6 %collective-permute-start = (bf16[1,128,1792]{1,2,0:T(8,128)(2,1)}, bf16[1,128,1792]{1,2,0:T(8,128)(2,1)S(1)}, u32[]{:S(2)}, u32[]{:S(2)}) collective-permute-start(bf16[1,128,1792]{1,2,0:T(8,128)(2,1)} %copy.10), channel_id=1, source_target_pairs={{16,0},{0,16},{17,1},{1,17},{18,2},{2,18},{19,3},{3,19},{20,4},{4,... | collective-permute-start | bytes 1376264 | tf_op jit(solution)/shard_map/ppermute | solution.py:20
  108.3 10.5 %collective-permute-start.12 = (bf16[128,1792]{0,1:T(8,128)(2,1)S(1)}, bf16[128,1792]{0,1:T(8,128)(2,1)S(1)}, u32[]{:S(2)}, u32[]{:S(2)}) collective-permute-start(bf16[128,1792]{0,1:T(8,128)(2,1)S(1)} %fusion.40), channel_id=1, source_target_pairs={{0,2},{2,0},{1,3},{3,1},{4,6},{6,4},{5,7},{7,5},{8,10},{10,8},{9,1... | collective-permute-start | bytes 1376264 | tf_op jit(solution)/shard_map/ppermute | solution.py:14
  108.4 11.8 %copy-start.7 = (bf16[1,128,1792]{1,2,0:T(8,128)(2,1)}, bf16[1,128,1792]{1,2,0:T(8,128)(2,1)S(1)}, u32[]{:S(2)}) copy-start(bf16[1,128,1792]{1,2,0:T(8,128)(2,1)S(1)} %collective-permute-done) | copy-start | bytes 1376260
  108.7 11.5 %collective-permute-start.1 = (bf16[128,1792]{0,1:T(8,128)(2,1)S(1)}, bf16[128,1792]{0,1:T(8,128)(2,1)S(1)}, u32[]{:S(2)}, u32[]{:S(2)}) collective-permute-start(bf16[128,1792]{0,1:T(8,128)(2,1)S(1)} %fusion), channel_id=1, source_target_pairs={{0,1},{1,0},{2,3},{3,2},{4,5},{5,4},{6,7},{7,6},{8,9},{9,8},{10,11... | collective-permute-start | bytes 1376264 | tf_op jit(solution)/shard_map/ppermute | solution.py:14
  120.2 1.9 collective-permute-start.13
  124.3 0.8 copy-start.2
  126.0 167.3 %reduce-scatter.2.cloned.1.call-start = ((), (), s32[]{:S(2)}) async-start(), calls=%async_computation.1 | async-start | bytes 3899392 | tf_op jit(solution)/shard_map/reduce_scatter | solution.py:98
  129.9 1.0 copy-start.9
  129.9 15.8 %copy-start.3 = (bf16[128,1792]{0,1:T(8,128)(2,1)S(1)}, bf16[128,1792]{0,1:T(8,128)(2,1)}, u32[]{:S(2)}) copy-start(bf16[128,1792]{0,1:T(8,128)(2,1)} %copy-done.2) | copy-start | bytes 1376260
  131.0 31.0 %copy-start.5 = (f32[4,128,448]{1,2,0:T(8,128)S(1)}, f32[4,128,448]{1,2,0:T(8,128)}, u32[]{:S(2)}) copy-start(f32[4,128,448]{1,2,0:T(8,128)} %copy-done.4) | copy-start | bytes 2752516
  131.0 12.8 %collective-permute-start.2 = (bf16[128,1792]{0,1:T(8,128)(2,1)S(1)}, bf16[128,1792]{0,1:T(8,128)(2,1)S(1)}, u32[]{:S(2)}, u32[]{:S(2)}) collective-permute-start(bf16[128,1792]{0,1:T(8,128)(2,1)S(1)} %copy-done.9), channel_id=1, source_target_pairs={{0,2},{2,0},{1,3},{3,1},{4,6},{6,4},{5,7},{7,5},{8,10},{10,8},{9,1... | collective-permute-start | bytes 1376264 | tf_op jit(solution)/shard_map/ppermute | solution.py:14
  145.1 12.0 %collective-permute-start.3 = (bf16[128,1792]{0,1:T(8,128)(2,1)S(1)}, bf16[128,1792]{0,1:T(8,128)(2,1)S(1)}, u32[]{:S(2)}, u32[]{:S(2)}) collective-permute-start(bf16[128,1792]{0,1:T(8,128)(2,1)S(1)} %fusion.8), channel_id=1, source_target_pairs={{0,4},{4,0},{1,5},{5,1},{2,6},{6,2},{3,7},{7,3},{8,12},{12,8},{9,1... | collective-permute-start | bytes 1376264 | tf_op jit(solution)/shard_map/ppermute | solution.py:14
  159.3 22.3 %collective-permute-start.4 = (bf16[128,1792]{0,1:T(8,128)(2,1)}, bf16[128,1792]{0,1:T(8,128)(2,1)}, u32[]{:S(2)}, u32[]{:S(2)}) collective-permute-start(bf16[128,1792]{0,1:T(8,128)(2,1)} %fusion.12), channel_id=1, source_target_pairs={{0,8},{8,0},{1,9},{9,1},{2,10},{10,2},{3,11},{11,3},{4,12},{12,4},... | collective-permute-start | bytes 1376264 | tf_op jit(solution)/shard_map/ppermute | solution.py:14
  161.9 19.7 %copy-start.8 = (bf16[1,128,1792]{1,2,0:T(8,128)(2,1)S(1)}, bf16[1,128,1792]{1,2,0:T(8,128)(2,1)}, u32[]{:S(2)}) copy-start(bf16[1,128,1792]{1,2,0:T(8,128)(2,1)} %copy-done.7) | copy-start | bytes 1376260
Sparse Core Ops, SparseCore 0:
  126.2 92.0 all-reduce.1
  223.2 70.1 reduce-scatter.1
where the time goes:
time: 302 us
  waiting for transfers between devices  227 us (75%)
  other arithmetic  22.3 us (7%)
  local copies, waits for them, and re-layouts  15.1 us (5%)
  between operations  14.3 us (5%)
  starting transfers between devices  14.1 us (5%)
  matrix products  8.92 us (3%)
    ppermute x12, waiting for transfers between devices, swapped(): return lax.ppermute(block, axis, route)  120 us
    reduce_scatter x1, waiting for transfers between devices, on_device(): lax.psum_scatter(weight_term, 'seq', scatter_dimension=0, tiled=True)  75.1 us
    psum x1, waiting for transfers between devices, on_device(): grad_block = lax.psum(block_term, 'seq')  31.9 us
    ppermute x12, starting transfers between devices, swapped(): return lax.ppermute(block, axis, route)  11.7 us
    unnamed x30, local copies, waits for them, and re-layouts  11 us
    convert_element_type x4, other arithmetic, mix_adjoint(): state = jnp.where(upper_side, as_upper, as_lower).astype(jnp.bfloat16)  8.65 us
    convert_element_type x5, other arithmetic, mix_forward(): state = jnp.where(upper_side, as_upper, as_lower).astype(jnp.bfloat16)  7.57 us
  transfers between devices with their start and end apart: 16, of which 13 were waited for; matrix products, arithmetic and copies ran while one was open for 10% of the time, Pallas kernels for 0%

commit v1 on v0

--- a/solution.py
+++ b/solution.py
@@ -100,7 +100,11 @@
     dblk = dblocked.reshape(-1, block_len, width)
     stored_blk = stored.reshape(-1, block_len, width)
     block_term = jnp.einsum("bid,bjd->ij", dblk, stored_blk, preferred_element_type=jnp.float32)
-    grad_block = lax.psum(block_term, "seq")
+    grad_block = block_term
+    for hop in (1, 2, 4, 8):
+        grad_block = grad_block + lax.ppermute(
+            grad_block, "seq", [(dev, dev ^ hop) for dev in range(16)]
+        )
     through = jnp.einsum("ij,bid->bjd", blocks, dblk, preferred_element_type=jnp.float32).reshape(
         rows_dev, width
     )

time: 302 us -> 216 us (0.72)
  waiting for transfers between devices: 227 us -> 139 us
  other arithmetic: 22.3 us -> 25.9 us
    reduce_scatter x1, waiting for transfers between devices: 75.1 us -> 0.01 us  [on_device(): lax.psum_scatter(weight_term, 'seq', scatter_dimension=0, tiled=True)]
    psum x1 -> x0, waiting for transfers between devices: 31.9 us -> none  [on_device(): grad_block = lax.psum(block_term, 'seq')]
    ppermute x0 -> x4, waiting for transfers between devices: none -> 24.8 us  [on_device(): lax.ppermute(grad_block, 'seq', [(dev, dev ^ hop) for dev in range(16)])]
    ppermute x12, waiting for transfers between devices: 120 us -> 114 us  [swapped(): return lax.ppermute(block, axis, route)]
    ppermute x0 -> x4, starting transfers between devices: none -> 3.37 us  [on_device(): lax.ppermute(grad_block, 'seq', [(dev, dev ^ hop) for dev in range(16)])]
    unnamed x30 -> x25, local copies, waits for them, and re-layouts: 11 us -> 8.51 us
  transfers between devices with their start and end apart: 16 -> 19, of which waited for: 13 -> 13; matrix products, arithmetic and copies ran while one was open for 10% -> 16% of each run, Pallas kernels for 0% -> 0%
where the time goes in v1:
time: 216 us; the launch traced here: 215 us
  waiting for transfers between devices  139 us (64%)
  other arithmetic  25.9 us (12%)
  starting transfers between devices  16.1 us (7%)
  between operations  14.3 us (7%)
  local copies, waits for them, and re-layouts  12.6 us (6%)
  matrix products  7.88 us (4%)
    ppermute x12, waiting for transfers between devices, swapped(): return lax.ppermute(block, axis, route)  114 us
    ppermute x4, waiting for transfers between devices, on_device(): lax.ppermute(grad_block, 'seq', [(dev, dev ^ hop) for dev in range(16)])  24.8 us
    convert_element_type x4, other arithmetic, mix_adjoint(): state = jnp.where(upper_side, as_upper, as_lower).astype(jnp.bfloat16)  11.6 us
    ppermute x12, starting transfers between devices, swapped(): return lax.ppermute(block, axis, route)  10.6 us
    unnamed x25, local copies, waits for them, and re-layouts  8.51 us
    convert_element_type x5, other arithmetic, mix_forward(): state = jnp.where(upper_side, as_upper, as_lower).astype(jnp.bfloat16)  7.57 us
    convert_element_type x2, other arithmetic, layer_forward(): (rows.astype(jnp.float32) + state.astype(jnp.float32)).astype(jnp.bfloat16)  5.86 us
  transfers between devices with their start and end apart: 19, of which 13 were waited for; matrix products, arithmetic and copies ran while one was open for 16% of the time, Pallas kernels for 0%

profile of v1, /device:TPU:0, one launch (start us, length us, event | category | flops | bytes accessed | tf_op | source)
XLA Modules:
  0.0 215.3 jit_solution(17736264543012038501)
XLA Ops:
  7.2 0.7 copy-done
  7.9 1.3 fusion.1
  9.8 1.3 slice_reduce_fusion.15
  11.2 1.3 fusion.20
  12.6 3.0 %collective-permute-start.7 = (bf16[128,1792]{0,1:T(8,128)(2,1)S(1)}, bf16[128,1792]{0,1:T(8,128)(2,1)S(1)}, u32[]{:S(2)}, u32[]{:S(2)}) collective-permute-start(bf16[128,1792]{0,1:T(8,128)(2,1)S(1)} %fusion.20), channel_id=1, source_target_pairs={{0,2},{2,0},{1,3},{3,1},{4,6},{6,4},{5,7},{7,5},{8,10},{10,8},{9,1... | collective-permute-start | bytes 1376264 | tf_op jit(solution)/shard_map/ppermute | solution.py:14
  15.5 10.8 %collective-permute-done.7 = bf16[128,1792]{0,1:T(8,128)(2,1)S(1)} collective-permute-done((bf16[128,1792]{0,1:T(8,128)(2,1)S(1)}, bf16[128,1792]{0,1:T(8,128)(2,1)S(1)}, u32[]{:S(2)}, u32[]{:S(2)}) %collective-permute-start.7) | collective-permute-done | bytes 458784 | tf_op jit(solution)/shard_map/ppermute | solution.py:14
  26.3 1.3 fusion.24
  27.7 1.9 collective-permute-start.8
  29.6 10.3 %collective-permute-done.8 = bf16[128,1792]{0,1:T(8,128)(2,1)S(1)} collective-permute-done((bf16[128,1792]{0,1:T(8,128)(2,1)S(1)}, bf16[128,1792]{0,1:T(8,128)(2,1)S(1)}, u32[]{:S(2)}, u32[]{:S(2)}) %collective-permute-start.8) | collective-permute-done | bytes 458784 | tf_op jit(solution)/shard_map/ppermute | solution.py:14
  39.8 1.3 fusion.28
  41.2 2.6 %collective-permute-start.9 = (bf16[128,1792]{0,1:T(8,128)(2,1)S(1)}, bf16[128,1792]{0,1:T(8,128)(2,1)}, u32[]{:S(2)}, u32[]{:S(2)}) collective-permute-start(bf16[128,1792]{0,1:T(8,128)(2,1)S(1)} %fusion.28), channel_id=1, source_target_pairs={{0,8},{8,0},{1,9},{9,1},{2,10},{10,2},{3,11},{11,3},{4,12},{12,4},... | collective-permute-start | bytes 1376264 | tf_op jit(solution)/shard_map/ppermute | solution.py:14
  43.7 1.0 copy.12
  44.7 1.5 collective-permute-start.5
  46.2 1.0 copy.13
  47.2 2.8 %copy.18 = bf16[1,1792,448]{2,1,0:T(8,128)(2,1)S(1)} copy(bf16[1,1792,448]{1,2,0:T(8,128)(2,1)} %param.11) | data formatting | bytes 3211264 | tf_op jit(solution)/shard_map/reshape;squeeze | solution.py:66
  50.0 13.3 %collective-permute-done.9 = bf16[128,1792]{0,1:T(8,128)(2,1)} collective-permute-done((bf16[128,1792]{0,1:T(8,128)(2,1)S(1)}, bf16[128,1792]{0,1:T(8,128)(2,1)}, u32[]{:S(2)}, u32[]{:S(2)}) %collective-permute-start.9) | collective-permute-done | bytes 458784 | tf_op jit(solution)/shard_map/ppermute | solution.py:14
  63.2 3.0 %add_convert_fusion.1 = bf16[128,1792]{0,1:T(8,128)(2,1)S(1)} fusion(bf16[128,1792]{0,1:T(8,128)(2,1)} %copy-done.8, bf16[128,1792]{0,1:T(8,128)(2,1)} %collective-permute-done.9, bf16[1,128,1792]{1,2,0:T(8,128)(2,1)} %copy.13, f32[1792]{0:T(1024)S(1)} %get-tuple-element.9, f32[1792]{0:T(1024)S(1)} %get-tuple-element.10, f32[1792]{0:T(1024)S(1)} %get-tuple-element.11, ...), kind=kLoop, calls=%fused_computation.109 | loop fusion | flops 3211264 | bytes 1863681 | tf_op jit(solution)/shard_map/convert_element_type | solution.py:64
  66.2 0.8 convolution_bitcast_fusion.1
  67.1 0.7 fusion.60
  68.0 0.9 copy-done.2
  69.1 22.5 %collective-permute-done.10 = bf16[128,1792]{0,1:T(8,128)(2,1)S(1)} collective-permute-done((bf16[128,1792]{0,1:T(8,128)(2,1)S(1)}, bf16[128,1792]{0,1:T(8,128)(2,1)S(1)}, u32[]{:S(2)}, u32[]{:S(2)}) %collective-permute-start.10) | collective-permute-done | bytes 458784 | tf_op jit(solution)/shard_map/ppermute | solution.py:14
  91.6 2.2 %fusion.36 = bf16[128,1792]{0,1:T(8,128)(2,1)} fusion(bf16[128,1792]{0,1:T(8,128)(2,1)S(1)} %collective-permute-done.10, bf16[128,1792]{0,1:T(8,128)(2,1)S(1)} %fusion.50, f32[1792]{0:T(1024)S(1)} %get-tuple-element.9, f32[1792]{0:T(1024)S(1)} %get-tuple-element.10, f32[1792]{0:T(1024)S(1)} %get-tuple-element.11, f32[1792]{0:T(1024)S(1)} %get-tuple-element.8, ...), kind=kLoop, calls=%fused_computation.89 | loop fusion | flops 2293760 | bytes 1404929 | tf_op jit(solution)/shard_map/convert_element_type | solution.py:47
  93.8 2.0 copy.10
  96.4 9.0 %collective-permute-done.11 = bf16[128,1792]{0,1:T(8,128)(2,1)} collective-permute-done((bf16[128,1792]{0,1:T(8,128)(2,1)}, bf16[128,1792]{0,1:T(8,128)(2,1)}, u32[]{:S(2)}, u32[]{:S(2)}) %collective-permute-start.11) | collective-permute-done | bytes 458784 | tf_op jit(solution)/shard_map/ppermute | solution.py:14
  105.5 3.6 %fusion.40 = bf16[128,1792]{0,1:T(8,128)(2,1)} fusion(bf16[128,1792]{0,1:T(8,128)(2,1)} %collective-permute-done.11, bf16[128,1792]{0,1:T(8,128)(2,1)} %fusion.36, f32[1792]{0:T(1024)S(1)} %get-tuple-element.12, f32[1792]{0:T(1024)S(1)} %get-tuple-element.13, f32[1792]{0:T(1024)S(1)} %get-tuple-element.14, f32[1792]{0:T(1024)S(1)} %get-tuple-element.23, ...), kind=kLoop, calls=%fused_computation.93 | loop fusion | flops 2293760 | bytes 1404929 | tf_op jit(solution)/shard_map/convert_element_type | solution.py:47
  109.0 0.8 copy-done.6
  109.8 1.1 fusion
  110.8 2.5 %fusion.59 = f32[4,448,448]{2,1,0:T(8,128)} fusion(bf16[128,4,448]{0,2,1:T(8,128)(2,1)S(1)} %bitcast.83, f32[128,4,448]{0,2,1:T(8,128)S(1)} %copy-done.5, bf16[128,4,448]{0,2,1:T(8,128)(2,1)S(1)} %bitcast.81), kind=kOutput, calls=%fused_computation.136 | convolution fusion | flops 207814656 | bytes 5046272 | tf_op jit(solution)/shard_map/tbi,tbo->bio/dot_general | solution.py:95
  113.4 6.3 %collective-permute-done.12 = bf16[128,1792]{0,1:T(8,128)(2,1)} collective-permute-done((bf16[128,1792]{0,1:T(8,128)(2,1)}, bf16[128,1792]{0,1:T(8,128)(2,1)}, u32[]{:S(2)}, u32[]{:S(2)}) %collective-permute-start.12) | collective-permute-done | bytes 458784 | tf_op jit(solution)/shard_map/ppermute | solution.py:14
  119.7 2.9 %fusion.44 = bf16[128,1792]{0,1:T(8,128)(2,1)S(1)} fusion(bf16[128,1792]{0,1:T(8,128)(2,1)} %collective-permute-done.12, bf16[128,1792]{0,1:T(8,128)(2,1)} %fusion.40, f32[1792]{0:T(1024)S(1)} %get-tuple-element.15, f32[1792]{0:T(1024)S(1)} %get-tuple-element.16, f32[1792]{0:T(1024)S(1)} %get-tuple-element.17, f32[1792]{0:T(1024)S(1)} %get-tuple-element.22, ...), kind=kLoop, calls=%fused_computation.97 | loop fusion | flops 2293760 | bytes 1404929 | tf_op jit(solution)/shard_map/convert_element_type | solution.py:47
  122.7 1.8 collective-permute-done.13
  124.5 2.9 %fusion.48 = (bf16[128,1792]{0,1:T(8,128)(2,1)S(1)}, bf16[128,1792]{0,1:T(8,128)(2,1)S(1)}) fusion(bf16[128,1792]{0,1:T(8,128)(2,1)S(1)} %collective-permute-done.13, bf16[128,1792]{0,1:T(8,128)(2,1)S(1)} %fusion.44, f32[1792]{0:T(1024)S(1)} %get-tuple-element.18, f32[1792]{0:T(1024)S(1)} %get-tuple-element.19, f32[1792]{0:T(1024)S(1)} %get-tuple-element.20, ...), kind=kLoop, calls=%fused_computation.101 | loop fusion | flops 4587520 | bytes 2781185 | tf_op jit(solution)/shard_map/convert_element_type | solution.py:47
  127.8 12.3 %collective-permute-done.2 = bf16[128,1792]{0,1:T(8,128)(2,1)S(1)} collective-permute-done((bf16[128,1792]{0,1:T(8,128)(2,1)S(1)}, bf16[128,1792]{0,1:T(8,128)(2,1)S(1)}, u32[]{:S(2)}, u32[]{:S(2)}) %collective-permute-start.2) | collective-permute-done | bytes 458784 | tf_op jit(solution)/shard_map/ppermute | solution.py:14
  140.1 1.3 fusion.8
  141.5 0.7 collective-permute-start.3
  142.5 1.2 collective-permute-done.14
  144.1 5.8 %collective-permute-done.15 = f32[128,128]{1,0:T(8,128)S(1)} collective-permute-done((f32[128,128]{1,0:T(8,128)S(1)}, f32[128,128]{1,0:T(8,128)S(1)}, u32[]{:S(2)}, u32[]{:S(2)}) %collective-permute-start.15) | collective-permute-done | bytes 65568 | tf_op jit(solution)/shard_map/ppermute | solution.py:105
  149.9 1.5 collective-permute-start.16
  151.7 17.8 %collective-permute-done.16 = f32[128,128]{1,0:T(8,128)S(1)} collective-permute-done((f32[128,128]{1,0:T(8,128)S(1)}, f32[128,128]{1,0:T(8,128)S(1)}, u32[]{:S(2)}, u32[]{:S(2)}) %collective-permute-start.16) | collective-permute-done | bytes 65568 | tf_op jit(solution)/shard_map/ppermute | solution.py:105
  169.5 1.4 collective-permute-start.17
  170.9 2.2 %fusion.12 = bf16[128,1792]{0,1:T(8,128)(2,1)} fusion(bf16[128,1792]{0,1:T(8,128)(2,1)S(1)} %collective-permute-done.3, bf16[128,1792]{0,1:T(8,128)(2,1)S(1)} %fusion.8, f32[1792]{0:T(1024)S(1)} %get-tuple-element.12, f32[1792]{0:T(1024)S(1)} %get-tuple-element.13, f32[1792]{0:T(1024)S(1)} %get-tuple-element.14, f32[1792]{0:T(1024)S(1)} %get-tuple-element.23, ...), kind=kLoop, calls=%fused_computation.65 | loop fusion | flops 2293760 | bytes 1404929 | tf_op jit(solution)/shard_map/convert_element_type | solution.py:33
  173.1 1.5 collective-permute-start.4
  174.8 1.0 copy.17
  175.8 0.6 add_bitcast_fusion
  176.5 27.3 %collective-permute-done.4 = bf16[128,1792]{0,1:T(8,128)(2,1)} collective-permute-done((bf16[128,1792]{0,1:T(8,128)(2,1)}, bf16[128,1792]{0,1:T(8,128)(2,1)}, u32[]{:S(2)}, u32[]{:S(2)}) %collective-permute-start.4) | collective-permute-done | bytes 458784 | tf_op jit(solution)/shard_map/ppermute | solution.py:14
  203.8 2.9 %add_convert_fusion.3 = bf16[128,1792]{0,1:T(8,128)(2,1)S(1)} fusion(bf16[128,1792]{0,1:T(8,128)(2,1)} %fusion.12, bf16[128,1792]{0,1:T(8,128)(2,1)} %collective-permute-done.4, bf16[1,128,1792]{1,2,0:T(8,128)(2,1)S(1)} %copy-done.7, f32[1792]{0:T(1024)S(1)} %get-tuple-element.9, f32[1792]{0:T(1024)S(1)} %get-tuple-element.10, ...), kind=kLoop, calls=%fused_computation.111 | loop fusion | flops 3211264 | bytes 1863681 | tf_op jit(solution)/shard_map/convert_element_type | solution.py:64
  206.6 0.9 add_convert_fusion.2
  207.5 1.0 copy.16
  (43 shorter events, 3.3 us)
Async XLA Ops:
  7.2 0.8 copy-start
  7.2 201.3 %reduce-scatter.2.cloned.1.call-start = ((), (), s32[]{:S(2)}) async-start(), calls=%async_computation.1 | async-start | bytes 3899392 | tf_op jit(solution)/shard_map/reduce_scatter | solution.py:98
  9.3 2.0 collective-permute-start.6
  11.2 32.5 %copy-start.9 = (bf16[1,128,1792]{2,1,0:T(8,128)(2,1)S(1)}, bf16[1,128,1792]{2,1,0:T(8,128)(2,1)}, u32[]{:S(2)}) copy-start(bf16[1,128,1792]{2,1,0:T(8,128)(2,1)} %param.7) | copy-start | bytes 1376260
  12.6 13.8 %collective-permute-start.7 = (bf16[128,1792]{0,1:T(8,128)(2,1)S(1)}, bf16[128,1792]{0,1:T(8,128)(2,1)S(1)}, u32[]{:S(2)}, u32[]{:S(2)}) collective-permute-start(bf16[128,1792]{0,1:T(8,128)(2,1)S(1)} %fusion.20), channel_id=1, source_target_pairs={{0,2},{2,0},{1,3},{3,1},{4,6},{6,4},{5,7},{7,5},{8,10},{10,8},{9,1... | collective-permute-start | bytes 1376264 | tf_op jit(solution)/shard_map/ppermute | solution.py:14
  26.3 19.9 %copy-start.1 = (bf16[1,128,1792]{2,1,0:T(8,128)(2,1)S(1)}, bf16[1,128,1792]{2,1,0:T(8,128)(2,1)}, u32[]{:S(2)}) copy-start(bf16[1,128,1792]{2,1,0:T(8,128)(2,1)} %param.8) | copy-start | bytes 1376260
  27.7 12.1 %collective-permute-start.8 = (bf16[128,1792]{0,1:T(8,128)(2,1)S(1)}, bf16[128,1792]{0,1:T(8,128)(2,1)S(1)}, u32[]{:S(2)}, u32[]{:S(2)}) collective-permute-start(bf16[128,1792]{0,1:T(8,128)(2,1)S(1)} %fusion.24), channel_id=1, source_target_pairs={{0,4},{4,0},{1,5},{5,1},{2,6},{6,2},{3,7},{7,3},{8,12},{12,8},{9,1... | collective-permute-start | bytes 1376264 | tf_op jit(solution)/shard_map/ppermute | solution.py:14
  41.2 8.8 %copy-start.8 = (bf16[128,1792]{0,1:T(8,128)(2,1)}, bf16[128,1792]{0,1:T(8,128)(2,1)S(1)}, u32[]{:S(2)}) copy-start(bf16[128,1792]{0,1:T(8,128)(2,1)S(1)} %fusion.28) | copy-start | bytes 1376260
  41.2 22.1 %collective-permute-start.9 = (bf16[128,1792]{0,1:T(8,128)(2,1)S(1)}, bf16[128,1792]{0,1:T(8,128)(2,1)}, u32[]{:S(2)}, u32[]{:S(2)}) collective-permute-start(bf16[128,1792]{0,1:T(8,128)(2,1)S(1)} %fusion.28), channel_id=1, source_target_pairs={{0,8},{8,0},{1,9},{9,1},{2,10},{10,2},{3,11},{11,3},{4,12},{12,4},... | collective-permute-start | bytes 1376264 | tf_op jit(solution)/shard_map/ppermute | solution.py:14
  44.7 22.3 %collective-permute-start.5 = (bf16[1,128,1792]{1,2,0:T(8,128)(2,1)}, bf16[1,128,1792]{1,2,0:T(8,128)(2,1)S(1)}, u32[]{:S(2)}, u32[]{:S(2)}) collective-permute-start(bf16[1,128,1792]{1,2,0:T(8,128)(2,1)} %copy.12), channel_id=1, source_target_pairs={{16,0},{0,16},{17,1},{1,17},{18,2},{2,18},{19,3},{3,19},{20,4},{4,... | collective-permute-start | bytes 1376264 | tf_op jit(solution)/shard_map/ppermute | solution.py:20
  67.1 0.9 copy-start.4
  68.0 0.9 copy-start.2
  69.0 22.6 %collective-permute-start.10 = (bf16[128,1792]{0,1:T(8,128)(2,1)S(1)}, bf16[128,1792]{0,1:T(8,128)(2,1)S(1)}, u32[]{:S(2)}, u32[]{:S(2)}) collective-permute-start(bf16[128,1792]{0,1:T(8,128)(2,1)S(1)} %fusion.50), channel_id=1, source_target_pairs={{0,8},{8,0},{1,9},{9,1},{2,10},{10,2},{3,11},{11,3},{4,12},{12,4},... | collective-permute-start | bytes 1376264 | tf_op jit(solution)/shard_map/ppermute | solution.py:14
  93.8 11.6 %collective-permute-start.11 = (bf16[128,1792]{0,1:T(8,128)(2,1)}, bf16[128,1792]{0,1:T(8,128)(2,1)}, u32[]{:S(2)}, u32[]{:S(2)}) collective-permute-start(bf16[128,1792]{0,1:T(8,128)(2,1)} %fusion.36), channel_id=1, source_target_pairs={{0,4},{4,0},{1,5},{5,1},{2,6},{6,2},{3,7},{7,3},{8,12},{12,8},{9,1... | collective-permute-start | bytes 1376264 | tf_op jit(solution)/shard_map/ppermute | solution.py:14
  95.8 15.0 %copy-start.5 = (f32[128,4,448]{0,2,1:T(8,128)S(1)}, f32[128,4,448]{0,2,1:T(8,128)}, u32[]{:S(2)}) copy-start(f32[128,4,448]{0,2,1:T(8,128)} %copy-done.4) | copy-start | bytes 2752516
  95.8 13.2 %collective-permute-start = (bf16[1,128,1792]{1,2,0:T(8,128)(2,1)}, bf16[1,128,1792]{1,2,0:T(8,128)(2,1)S(1)}, u32[]{:S(2)}, u32[]{:S(2)}) collective-permute-start(bf16[1,128,1792]{1,2,0:T(8,128)(2,1)} %copy.10), channel_id=1, source_target_pairs={{16,0},{0,16},{17,1},{1,17},{18,2},{2,18},{19,3},{3,19},{20,4},{4,... | collective-permute-start | bytes 1376264 | tf_op jit(solution)/shard_map/ppermute | solution.py:20
  109.0 10.7 %collective-permute-start.12 = (bf16[128,1792]{0,1:T(8,128)(2,1)}, bf16[128,1792]{0,1:T(8,128)(2,1)}, u32[]{:S(2)}, u32[]{:S(2)}) collective-permute-start(bf16[128,1792]{0,1:T(8,128)(2,1)} %fusion.40), channel_id=1, source_target_pairs={{0,2},{2,0},{1,3},{3,1},{4,6},{6,4},{5,7},{7,5},{8,10},{10,8},{9,1... | collective-permute-start | bytes 1376264 | tf_op jit(solution)/shard_map/ppermute | solution.py:14
  109.0 0.8 copy-start.6
  110.8 11.9 %collective-permute-start.1 = (bf16[128,1792]{0,1:T(8,128)(2,1)}, bf16[128,1792]{0,1:T(8,128)(2,1)}, u32[]{:S(2)}, u32[]{:S(2)}) collective-permute-start(bf16[128,1792]{0,1:T(8,128)(2,1)} %fusion), channel_id=1, source_target_pairs={{0,1},{1,0},{2,3},{3,2},{4,5},{5,4},{6,7},{7,6},{8,9},{9,8},{10,11... | collective-permute-start | bytes 1376264 | tf_op jit(solution)/shard_map/ppermute | solution.py:14
  122.6 1.9 collective-permute-start.13
  127.4 12.7 %collective-permute-start.2 = (bf16[128,1792]{0,1:T(8,128)(2,1)S(1)}, bf16[128,1792]{0,1:T(8,128)(2,1)S(1)}, u32[]{:S(2)}, u32[]{:S(2)}) collective-permute-start(bf16[128,1792]{0,1:T(8,128)(2,1)S(1)} %get-tuple-element.25), channel_id=1, source_target_pairs={{0,2},{2,0},{1,3},{3,1},{4,6},{6,4},{5,7},{7,5},{8,10},{10,8},{9,1... | collective-permute-start | bytes 1376264 | tf_op jit(solution)/shard_map/ppermute | solution.py:14
  141.5 29.5 %collective-permute-start.3 = (bf16[128,1792]{0,1:T(8,128)(2,1)S(1)}, bf16[128,1792]{0,1:T(8,128)(2,1)S(1)}, u32[]{:S(2)}, u32[]{:S(2)}) collective-permute-start(bf16[128,1792]{0,1:T(8,128)(2,1)S(1)} %fusion.8), channel_id=1, source_target_pairs={{0,4},{4,0},{1,5},{5,1},{2,6},{6,2},{3,7},{7,3},{8,12},{12,8},{9,1... | collective-permute-start | bytes 1376264 | tf_op jit(solution)/shard_map/ppermute | solution.py:14
  142.4 32.2 %copy-start.3 = (f32[4,128,448]{1,2,0:T(8,128)S(1)}, f32[4,128,448]{1,2,0:T(8,128)}, u32[]{:S(2)}) copy-start(f32[4,128,448]{1,2,0:T(8,128)} %copy-done.2) | copy-start | bytes 2752516
  142.5 1.3 collective-permute-start.14
  143.8 6.1 %collective-permute-start.15 = (f32[128,128]{1,0:T(8,128)S(1)}, f32[128,128]{1,0:T(8,128)S(1)}, u32[]{:S(2)}, u32[]{:S(2)}) collective-permute-start(f32[128,128]{1,0:T(8,128)S(1)} %add.148), channel_id=1, source_target_pairs={{0,2},{1,3},{2,0},{3,1},{4,6},{5,7},{6,4},{7,5},{8,10},{9,11},{10,... | collective-permute-start | bytes 196616 | tf_op jit(solution)/shard_map/ppermute | solution.py:105
  149.9 19.5 %collective-permute-start.16 = (f32[128,128]{1,0:T(8,128)S(1)}, f32[128,128]{1,0:T(8,128)S(1)}, u32[]{:S(2)}, u32[]{:S(2)}) collective-permute-start(f32[128,128]{1,0:T(8,128)S(1)} %add.149), channel_id=1, source_target_pairs={{0,4},{1,5},{2,6},{3,7},{4,0},{5,1},{6,2},{7,3},{8,12},{9,13},{10,... | collective-permute-start | bytes 196616 | tf_op jit(solution)/shard_map/ppermute | solution.py:105
  169.5 6.3 %collective-permute-start.17 = (f32[128,128]{1,0:T(8,128)S(1)}, f32[128,128]{1,0:T(8,128)S(1)}, u32[]{:S(2)}, u32[]{:S(2)}) collective-permute-start(f32[128,128]{1,0:T(8,128)S(1)} %add.150), channel_id=1, source_target_pairs={{0,8},{1,9},{2,10},{3,11},{4,12},{5,13},{6,14},{7,15},{8,0},{9,1},... | collective-permute-start | bytes 196616 | tf_op jit(solution)/shard_map/ppermute | solution.py:105
  173.1 30.6 %collective-permute-start.4 = (bf16[128,1792]{0,1:T(8,128)(2,1)}, bf16[128,1792]{0,1:T(8,128)(2,1)}, u32[]{:S(2)}, u32[]{:S(2)}) collective-permute-start(bf16[128,1792]{0,1:T(8,128)(2,1)} %fusion.12), channel_id=1, source_target_pairs={{0,8},{8,0},{1,9},{9,1},{2,10},{10,2},{3,11},{11,3},{4,12},{12,4},... | collective-permute-start | bytes 1376264 | tf_op jit(solution)/shard_map/ppermute | solution.py:14
  174.7 29.1 %copy-start.7 = (bf16[1,128,1792]{1,2,0:T(8,128)(2,1)S(1)}, bf16[1,128,1792]{1,2,0:T(8,128)(2,1)}, u32[]{:S(2)}) copy-start(bf16[1,128,1792]{1,2,0:T(8,128)(2,1)} %copy-done.6) | copy-start | bytes 1376260
Sparse Core Ops, SparseCore 0:
  113.5 91.3 reduce-scatter.1
